TPU v7x, 32 devices: a whole 2x2x4 slice. The times are simulated.
32 devices in a mesh: dp: 8 (over z, x), sect: 4 (over y, core).
Axes of the slice: x: 2, y: 2, z: 4, core: 2. Of those that a mesh axis runs over, the one named last changes fastest.
Arguments:
- queries: bfloat16 [8, 16, 8192], P('dp', None, 'sect'), may hold values from -5 to 5
- keys: bfloat16 [8, 16, 8192], P('dp', None, 'sect'), may hold values from -5 to 5
- values: bfloat16 [8, 16, 8192], P('dp', None, 'sect'), may hold values from -6 to 6
- residual: bfloat16 [8, 16, 8192], P('dp'), may hold values from -6 to 6
- labels: int32 [8, 16], P('dp'), may hold values from 0 to 2, as said below
- slot_modality: int32 [4], replicated, may hold values from 0 to 2, as said below
- gains: float32 [3, 8192], replicated, may hold values from 0.1 to 1.9
- up_weight: bfloat16 [4, 11008, 8192], P('sect', 'dp'), may hold values from -0.0625 to 0.0625
- down_weight: bfloat16 [4, 11008, 8192], P('sect', 'dp'), may hold values from -0.0546875 to 0.0546875
- cotangent: bfloat16 [8, 16, 8192], P('dp'), may hold values from -6 to 6
Outputs:
- output: bfloat16 [8, 16, 8192], P('dp', 'sect')
- residual_grad: bfloat16 [8, 16, 8192], P('dp', 'sect')
- query_grad: bfloat16 [8, 16, 8192], P('dp', None, 'sect')
- key_grad: bfloat16 [8, 16, 8192], P('dp', None, 'sect')
- value_grad: bfloat16 [8, 16, 8192], P('dp', None, 'sect')
- up_grad: bfloat16 [4, 11008, 8192], P('sect', 'dp')
- down_grad: bfloat16 [4, 11008, 8192], P('sect', 'dp')
- gain_grad: float32 [3, 8192], replicated
Inputs may be any that keep to these rules, and one draw needn't show every extreme that they name: `labels`: every sequence holds exactly 8 text tokens (label 0); its other tokens are image or speech. `slot_modality`: text owns two slots, image one, speech one.
All inputs are finite; a program needn't handle non-finite values.
Results may differ from a plain program's by a relative error of at most 0.015.
The roundings to bfloat16 on the way count: a program that leaves them out, or rounds other values in their place, can miss the bound.
Values may be sent and summed in bfloat16 or wider, within the bound.
A program may use at most 192 MiB of HBM per device.

v0:
```python
import jax
import jax.numpy as jnp
from jax import lax
from jax.sharding import PartitionSpec as P

HD = 128
MODALITIES = 3


def causal_forward(queries, keys, values):
    seq_count, length, width = queries.shape
    head_count = width // HD
    query_f = queries.astype(jnp.float32).reshape(seq_count, length, head_count, HD)
    key_f = keys.astype(jnp.float32).reshape(seq_count, length, head_count, HD)
    value_f = values.astype(jnp.float32).reshape(seq_count, length, head_count, HD)
    scores = jnp.einsum("sqhd,skhd->shqk", query_f, key_f) * HD ** (-0.5)
    position = jnp.arange(length)
    causal = position[:, None] >= position[None, :]
    scores = jnp.where(causal, scores, -1e30)
    probs = jax.nn.softmax(scores, axis=-1)
    probs_b = probs.astype(jnp.bfloat16)
    attended = jnp.einsum("shqk,skhd->sqhd", probs_b.astype(jnp.float32), value_f)
    return (attended.astype(jnp.bfloat16).reshape(seq_count, length, width), probs, probs_b)


def causal_backward(grad_out, queries, keys, values, attended, probs, probs_b):
    seq_count, length, width = queries.shape
    head_count = width // HD
    shape = (seq_count, length, head_count, HD)
    grad_f = grad_out.astype(jnp.float32).reshape(shape)
    query_f = queries.astype(jnp.float32).reshape(shape)
    key_f = keys.astype(jnp.float32).reshape(shape)
    value_f = values.astype(jnp.float32).reshape(shape)
    attended_f = attended.astype(jnp.float32).reshape(shape)
    value_grad = jnp.einsum("shqk,sqhd->skhd", probs_b.astype(jnp.float32), grad_f).astype(
        jnp.bfloat16
    )
    dprob = jnp.einsum("sqhd,skhd->shqk", grad_f, value_f)
    delta = jnp.einsum("sqhd,sqhd->shq", grad_f, attended_f)
    dscore = (
        (probs * (dprob - delta[..., None]) * HD ** (-0.5)).astype(jnp.bfloat16).astype(jnp.float32)
    )
    query_grad = jnp.einsum("shqk,skhd->sqhd", dscore, key_f).astype(jnp.bfloat16)
    key_grad = jnp.einsum("shqk,sqhd->skhd", dscore, query_f).astype(jnp.bfloat16)
    return (
        query_grad.reshape(seq_count, length, width),
        key_grad.reshape(seq_count, length, width),
        value_grad.reshape(seq_count, length, width),
    )


def spread(block):
    return lax.all_gather(block, "dp", axis=0, tiled=True)


def collect(term_fn, count):
    return lax.psum_scatter(
        term_fn(jnp.int32(0), lax.axis_size("dp") * count), "dp", scatter_dimension=0, tiled=True
    )


def pack(full_rows, selector):
    return jnp.dot(selector, full_rows, preferred_element_type=jnp.float32).astype(jnp.bfloat16)


def unpack(sums, selector):
    return jnp.dot(selector.astype(jnp.float32).T, sums, precision=lax.Precision.HIGHEST)


def over_slots(partial_rows):
    return lax.psum(partial_rows, "sect")


def contract_last(left, right):
    return lax.dot_general(
        left, right, (((1,), (1,)), ((), ())), preferred_element_type=jnp.float32
    )


def contract_first(left, right):
    return lax.dot_general(
        left, right, (((0,), (0,)), ((), ())), preferred_element_type=jnp.float32
    )


def on_device(
    queries, keys, values, residual, labels, slot_modality, gains, up_weight, down_weight, cotangent
):
    attended_block, probs, probs_b = causal_forward(queries, keys, values)
    attended = lax.all_gather(attended_block, "sect", axis=2, tiled=True)
    hidden = (residual.astype(jnp.float32) + attended.astype(jnp.float32)).astype(jnp.bfloat16)[0]
    hidden_f = hidden.astype(jnp.float32)
    length = hidden.shape[0]
    token_labels = labels[0]
    onehot = (token_labels[:, None] == jnp.arange(MODALITIES)[None, :]).astype(jnp.float32)
    gain_rows = jnp.dot(onehot, gains, precision=lax.Precision.HIGHEST)
    inverse = lax.rsqrt(jnp.mean(hidden_f * hidden_f, axis=-1, keepdims=True) + 1e-05)
    normed_f = hidden_f * inverse
    normed = (normed_f * gain_rows).astype(jnp.bfloat16)
    slot_index = lax.axis_index("sect")
    slot_count = lax.axis_size("sect")
    modality = jnp.sum(jnp.where(jnp.arange(slot_count) == slot_index, slot_modality, 0))
    keep_mask = token_labels == modality
    rank_of = jnp.cumsum(keep_mask.astype(jnp.int32)) - 1
    capacity = length // 2
    selector = ((rank_of[None, :] == jnp.arange(capacity)[:, None]) & keep_mask[None, :]).astype(
        jnp.bfloat16
    )
    up_local = up_weight[0]
    down_local = down_weight[0]
    own_rows = pack(normed, selector)
    count = own_rows.shape[0]
    token_rows = spread(own_rows)
    preact = contract_last(token_rows, up_local)
    activated = jax.nn.silu(preact).astype(jnp.bfloat16)

    def output_term(start, number):
        return jnp.dot(activated, down_local, preferred_element_type=jnp.float32)

    ffn = over_slots(unpack(collect(output_term, count), selector))
    output_full = (hidden_f + ffn).astype(jnp.bfloat16)
    quarter = length // slot_count
    output = lax.dynamic_slice_in_dim(output_full, slot_index * quarter, quarter, 0)[None]
    grad_full = cotangent[0]
    grad_rows = spread(pack(grad_full, selector))
    back = contract_last(grad_rows, down_local)
    sigma = jax.nn.sigmoid(preact)
    pre_grad = (back * sigma * (1.0 + preact * (1.0 - sigma))).astype(jnp.bfloat16)
    down_grad = contract_first(activated, grad_rows).astype(jnp.bfloat16)[None]
    up_grad = contract_first(pre_grad, token_rows).astype(jnp.bfloat16)[None]

    def norm_term(start, number):
        return jnp.dot(pre_grad, up_local, preferred_element_type=jnp.float32)

    norm_grad = over_slots(unpack(collect(norm_term, count), selector))
    scaled = norm_grad * gain_rows
    hidden_grad = grad_full.astype(jnp.float32) + inverse * (
        scaled - normed_f * jnp.mean(scaled * normed_f, axis=-1, keepdims=True)
    )
    residual_full = hidden_grad.astype(jnp.bfloat16)
    residual_grad = lax.dynamic_slice_in_dim(residual_full, slot_index * quarter, quarter, 0)[None]
    gain_part = jnp.dot(onehot.T, norm_grad * normed_f, precision=lax.Precision.HIGHEST)
    gain_grad = lax.psum(gain_part, "dp")
    block_width = queries.shape[2]
    grad_block = lax.dynamic_slice_in_dim(residual_full, slot_index * block_width, block_width, 1)[
        None
    ]
    query_grad, key_grad, value_grad = causal_backward(
        grad_block, queries, keys, values, attended_block, probs, probs_b
    )
    return (output, residual_grad, query_grad, key_grad, value_grad, up_grad, down_grad, gain_grad)


def solution(mesh):
    in_specs = (
        P("dp", None, "sect"),
        P("dp", None, "sect"),
        P("dp", None, "sect"),
        P("dp", None, None),
        P("dp", None),
        P(),
        P(),
        P("sect", "dp", None),
        P("sect", "dp", None),
        P("dp", None, None),
    )
    out_specs = (
        P("dp", "sect", None),
        P("dp", "sect", None),
        P("dp", None, "sect"),
        P("dp", None, "sect"),
        P("dp", None, "sect"),
        P("sect", "dp", None),
        P("sect", "dp", None),
        P(),
    )
    return jax.shard_map(
        on_device, mesh=mesh, in_specs=in_specs, out_specs=out_specs, check_vma=False
    )
```

profile of v0, /device:TPU:1, one launch (start us, length us, event | category | flops | bytes accessed | tf_op | source)
XLA Modules:
  0.0 390.3 jit_solution(13436349189762441844)
XLA Ops:
  7.3 1.3 fusion.69
  8.5 1.3 compare_bitcast_fusion
  10.1 0.9 copy.58
  11.0 0.9 copy.59
  11.9 0.9 copy.60
  13.6 0.6 copy-done.9
  14.2 7.1 %all_gather.9 = bf16[1,16,8192]{2,1,0:T(8,128)(2,1)S(1)} all-gather(bf16[1,16,2048]{2,1,0:T(8,128)(2,1)S(1)} %copy_bitcast_fusion.3), channel_id=1, replica_groups=mesh['dp'=8,'sect'=4] {'sect'}, dimensions={2}, use_global_device_ids=true | all-gather | bytes 327680 | tf_op jit(solution)/shard_map/all_gather | solution.py:90
  21.3 1.8 fusion.72
  23.3 1.1 fusion.50
  24.4 0.9 convolution_convert_fusion.3
  25.4 1.8 convolution_convert_fusion.2
  27.3 37.6 %all-gather.3.cloned.1.call-done = bf16[64,8192]{1,0:T(8,128)(2,1)} async-done(((bf16[8,8192]{1,0:T(8,128)(2,1)}), bf16[64,8192]{1,0:T(8,128)(2,1)}) %all-gather.3.cloned.1.call-update) | async-done | bytes 1048592 | tf_op jit(solution)/shard_map/all_gather | solution.py:53
  64.8 12.8 %fusion.9 = f32[64,1376]{1,0:T(8,128)S(1)} fusion(bf16[64,8192]{1,0:T(8,128)(2,1)} %all-gather.3.cloned.1.call-done, bf16[1,1376,8192]{2,1,0:T(8,128)(2,1)} %param.17), kind=kOutput, calls=%fused_computation.11 | convolution fusion | flops 1442840576 | bytes 23945216 | tf_op jit(solution)/shard_map/dot_general | solution.py:75
  77.6 28.9 %all-gather.5.cloned.1.call-done = bf16[64,8192]{1,0:T(8,128)(2,1)} async-done(((bf16[8,8192]{1,0:T(8,128)(2,1)}), bf16[64,8192]{1,0:T(8,128)(2,1)}) %all-gather.5.cloned.1.call-update) | async-done | bytes 1048592 | tf_op jit(solution)/shard_map/all_gather | solution.py:53
  106.5 11.5 %fusion.17 = bf16[64,1376]{1,0:T(8,128)(2,1)S(1)} fusion(bf16[64,8192]{1,0:T(8,128)(2,1)} %all-gather.5.cloned.1.call-done, bf16[1,1376,8192]{2,1,0:T(8,128)(2,1)} %param.18, f32[64,1376]{1,0:T(8,128)S(1)} %fusion.9), kind=kOutput, calls=%fused_computation.17 | convolution fusion | flops 1443633152 | bytes 24121344 | tf_op jit(solution)/shard_map/dot_general | solution.py:75
  118.0 12.9 %fusion.7 = f32[64,8192]{1,0:T(8,128)} fusion(bf16[64,1376]{1,0:T(8,128)(2,1)S(1)} %fusion.17, bf16[1,1376,8192]{2,1,0:T(8,128)(2,1)} %param.17), kind=kOutput, calls=%fused_computation.9 | convolution fusion | flops 1442840576 | bytes 24817664 | tf_op jit(solution)/shard_map/dot_general | solution.py:133
  131.2 12.9 %fusion.5 = f32[64,8192]{1,0:T(8,128)} fusion(bf16[1,1376,8192]{2,1,0:T(8,128)(2,1)} %param.18, f32[64,1376]{1,0:T(8,128)S(1)} %fusion.9), kind=kOutput, calls=%fused_computation.7 | convolution fusion | flops 1443280896 | bytes 24993792 | tf_op jit(solution)/shard_map/dot_general | solution.py:118
  144.1 54.1 %reduce-scatter.5.cloned.1.call-done = f32[8,8192]{1,0:T(8,128)} async-done(((f32[64,8192]{1,0:T(8,128)}), f32[8,8192]{1,0:T(8,128)}) %reduce-scatter.5.cloned.1.call-update) | async-done | bytes 262160 | tf_op jit(solution)/shard_map/reduce_scatter | solution.py:57
  198.3 2.2 fusion.54
  200.5 69.3 %reduce-scatter.3.cloned.1.call-done = f32[8,8192]{1,0:T(8,128)} async-done(((f32[64,8192]{1,0:T(8,128)}), f32[8,8192]{1,0:T(8,128)}) %reduce-scatter.3.cloned.1.call-update) | async-done | bytes 262160 | tf_op jit(solution)/shard_map/reduce_scatter | solution.py:57
  269.7 2.2 fusion.57
  272.0 11.2 %fusion.1 = bf16[1,1376,8192]{2,1,0:T(8,128)(2,1)} fusion(bf16[64,1376]{1,0:T(8,128)(2,1)S(1)} %fusion.17, bf16[64,8192]{1,0:T(8,128)(2,1)S(1)} %copy-done.2), kind=kOutput, calls=%fused_computation.3 | convolution fusion | flops 1454112768 | bytes 23769088 | tf_op jit(solution)/shard_map/dot_general | solution.py:81
  283.3 11.2 %fusion.2 = bf16[1,1376,8192]{2,1,0:T(8,128)(2,1)} fusion(bf16[64,8192]{1,0:T(8,128)(2,1)S(1)} %copy-done.3, f32[64,1376]{1,0:T(8,128)S(1)} %fusion.9), kind=kOutput, calls=%fused_computation.4 | convolution fusion | flops 1454553088 | bytes 23945216 | tf_op jit(solution)/shard_map/dot_general | solution.py:81
  294.5 14.2 %all-reduce.6.cloned.1.call-done = (f32[16,8192]{1,0:T(8,128)}, f32[16,8192]{1,0:T(8,128)}) async-done(((f32[16,8192]{1,0:T(8,128)}, f32[16,8192]{1,0:T(8,128)}), (f32[16,8192]{1,0:T(8,128)}, f32[16,8192]{1,0:T(8,128)})) %all-reduce.6.cloned.1.call-update) | async-done | bytes 1048592 | tf_op jit(solution)/shard_map/psum | solution.py:71
  308.7 1.3 multiply_reduce_fusion
  310.0 2.1 fusion.29
  312.3 0.7 dynamic-slice_bitcast_fusion
  313.7 1.7 fusion.38
  315.5 0.7 copy_bitcast_fusion
  316.3 0.6 copy.91
  317.0 64.9 %all-reduce.4.cloned.1.call-done = f32[3,8192]{1,0:T(4,128)} async-done(((f32[3,8192]{1,0:T(4,128)}), f32[3,8192]{1,0:T(4,128)}) %all-reduce.4.cloned.1.call-update) | async-done | bytes 98320 | tf_op jit(solution)/shard_map/psum | solution.py:143
  381.9 1.6 copy.95
  (78 shorter events, 3.0 us)
Async XLA Ops:
  7.2 16.2 %copy-start = (f32[3,8192]{1,0:T(4,128)S(1)}, f32[3,8192]{1,0:T(4,128)}, u32[]{:S(2)}) copy-start(f32[3,8192]{1,0:T(4,128)} %param.16) | copy-start | bytes 294916
  7.2 57.6 %all-gather.3.cloned.1.call-start = ((), (), s32[]{:S(2)}) async-start(), calls=%async_computation.2 | async-start | bytes 1179648 | tf_op jit(solution)/shard_map/all_gather | solution.py:53
  9.9 67.7 %copy-start.15 = (pred[16]{0:T(512)(128)(4,1)}, pred[16]{0:T(512)(128)(4,1)S(1)}, u32[]{:S(2)}) copy-start(pred[16]{0:T(512)(128)(4,1)S(1)} %get-tuple-element.16) | copy-start | bytes 52
  10.1 67.5 %copy-start.13 = (s32[16]{0:T(128)}, s32[16]{0:T(128)S(1)}, u32[]{:S(2)}) copy-start(s32[16]{0:T(128)S(1)} %add_reduce_fusion) | copy-start | bytes 196
  11.0 2.7 copy-start.7
  11.8 1.8 copy-start.5
  12.7 0.6 copy-start.11
  13.0 10.2 %copy-start.20 = (f32[16,16,16]{1,2,0:T(8,128)}, f32[16,16,16]{1,2,0:T(8,128)S(1)}, u32[]{:S(2)}) copy-start(f32[16,16,16]{1,2,0:T(8,128)S(1)} %get-tuple-element.19) | copy-start | bytes 49156
  13.0 64.6 %copy-start.22 = (f32[16,16]{1,0:T(8,128)}, f32[16,16]{1,0:T(8,128)S(1)}, u32[]{:S(2)}) copy-start(f32[16,16]{1,0:T(8,128)S(1)} %get-tuple-element.18) | copy-start | bytes 3076
  13.6 0.6 copy-start.9
  23.3 54.3 %copy-start.17 = (f32[16]{0:T(128)}, f32[16]{0:T(128)S(1)}, u32[]{:S(2)}) copy-start(f32[16]{0:T(128)S(1)} %add_rsqrt_fusion) | copy-start | bytes 196
  25.4 81.2 %all-gather.5.cloned.1.call-start = ((), (), s32[]{:S(2)}) async-start(), calls=%async_computation.4 | async-start | bytes 1179648 | tf_op jit(solution)/shard_map/all_gather | solution.py:53
  27.2 171.1 %reduce-scatter.5.cloned.1.call-start = ((), (), s32[]{:S(2)}) async-start(), calls=%async_computation.5 | async-start | bytes 2359296 | tf_op jit(solution)/shard_map/reduce_scatter | solution.py:57
  130.9 67.4 %copy-start.14 = (s32[16]{0:T(128)S(1)}, s32[16]{0:T(128)}, u32[]{:S(2)}) copy-start(s32[16]{0:T(128)} %copy-done.13) | copy-start | bytes 196
  130.9 67.4 %copy-start.16 = (pred[16]{0:T(512)(128)(4,1)S(1)}, pred[16]{0:T(512)(128)(4,1)}, u32[]{:S(2)}) copy-start(pred[16]{0:T(512)(128)(4,1)} %copy-done.15) | copy-start | bytes 52
  130.9 141.1 %copy-start.2 = (bf16[64,8192]{1,0:T(8,128)(2,1)S(1)}, bf16[64,8192]{1,0:T(8,128)(2,1)}, u32[]{:S(2)}) copy-start(bf16[64,8192]{1,0:T(8,128)(2,1)} %all-gather.3.cloned.1.call-done) | copy-start | bytes 3145732
  130.9 152.3 %copy-start.3 = (bf16[64,8192]{1,0:T(8,128)(2,1)S(1)}, bf16[64,8192]{1,0:T(8,128)(2,1)}, u32[]{:S(2)}) copy-start(bf16[64,8192]{1,0:T(8,128)(2,1)} %all-gather.5.cloned.1.call-done) | copy-start | bytes 3145732
  130.9 138.8 %reduce-scatter.3.cloned.1.call-start = ((), (), s32[]{:S(2)}) async-start(), calls=%async_computation.3 | async-start | bytes 2359296 | tf_op jit(solution)/shard_map/reduce_scatter | solution.py:57
  144.1 164.6 %all-reduce.6.cloned.1.call-start = ((), (), s32[]{:S(2)}) async-start(), calls=%async_computation.7 | async-start | bytes 2097152 | tf_op jit(solution)/shard_map/psum | solution.py:71
  271.9 111.6 %copy-start.1 = (f32[3,8192]{1,0:T(4,128)S(1)}, f32[3,8192]{1,0:T(4,128)}, u32[]{:S(2)}) copy-start(f32[3,8192]{1,0:T(4,128)} %param.16) | copy-start | bytes 294916
  271.9 110.0 %all-reduce.4.cloned.1.call-start = ((), (), s32[]{:S(2)}) async-start(), calls=%async_computation.6 | async-start | bytes 262144 | tf_op jit(solution)/shard_map/psum | solution.py:143
  283.2 25.5 %copy-start.18 = (f32[16]{0:T(128)S(1)}, f32[16]{0:T(128)}, u32[]{:S(2)}) copy-start(f32[16]{0:T(128)} %copy-done.17) | copy-start | bytes 196
  283.2 26.8 %copy-start.19 = (s32[1,16]{1,0:T(1,128)S(1)}, s32[1,16]{1,0:T(1,128)}, u32[]{:S(2)}) copy-start(s32[1,16]{1,0:T(1,128)} %param.14) | copy-start | bytes 196
  283.2 28.9 %copy-start.4 = (bf16[1,16,8192]{2,1,0:T(8,128)(2,1)S(1)}, bf16[1,16,8192]{2,1,0:T(8,128)(2,1)}, u32[]{:S(2)}) copy-start(bf16[1,16,8192]{2,1,0:T(8,128)(2,1)} %param.19) | copy-start | bytes 786436
  283.2 29.9 %copy-start.10 = (bf16[16,16,128]{2,1,0:T(8,128)(2,1)S(1)}, bf16[16,16,128]{2,1,0:T(8,128)(2,1)}, u32[]{:S(2)}) copy-start(bf16[16,16,128]{2,1,0:T(8,128)(2,1)} %copy-done.9) | copy-start | bytes 196612
  283.2 30.0 %copy-start.21 = (f32[16,16,16]{1,2,0:T(8,128)S(1)}, f32[16,16,16]{1,2,0:T(8,128)}, u32[]{:S(2)}) copy-start(f32[16,16,16]{1,2,0:T(8,128)} %copy-done.20) | copy-start | bytes 49156
  283.2 30.0 %copy-start.23 = (f32[16,16]{1,0:T(8,128)S(1)}, f32[16,16]{1,0:T(8,128)}, u32[]{:S(2)}) copy-start(f32[16,16]{1,0:T(8,128)} %copy-done.22) | copy-start | bytes 3076
  283.2 30.2 %copy-start.12 = (bf16[2,8,16,128]{3,2,1,0:T(8,128)(2,1)S(1)}, bf16[2,8,16,128]{3,2,1,0:T(8,128)(2,1)}, u32[]{:S(2)}) copy-start(bf16[2,8,16,128]{3,2,1,0:T(8,128)(2,1)} %copy-done.11) | copy-start | bytes 196612
  283.2 30.3 %copy-start.8 = (bf16[2,8,16,128]{3,2,1,0:T(8,128)(2,1)S(1)}, bf16[2,8,16,128]{3,2,1,0:T(8,128)(2,1)}, u32[]{:S(2)}) copy-start(bf16[2,8,16,128]{3,2,1,0:T(8,128)(2,1)} %copy-done.7) | copy-start | bytes 196612
  283.3 32.9 %copy-start.6 = (bf16[2,8,16,128]{3,2,1,0:T(8,128)(2,1)S(1)}, bf16[2,8,16,128]{3,2,1,0:T(8,128)(2,1)}, u32[]{:S(2)}) copy-start(bf16[2,8,16,128]{3,2,1,0:T(8,128)(2,1)} %copy-done.5) | copy-start | bytes 196612
Sparse Core Ops, SparseCore 0:
  25.5 39.2 all-gather.2
  67.5 38.9 all-gather.4
  131.0 67.1 reduce-scatter.4
  202.2 67.4 reduce-scatter.2
  272.0 36.5 all-reduce.5
  312.4 69.4 all-reduce.3
where the time goes:
time: 393 us; the launch traced here: 390 us
  waiting for transfers between devices  269 us (68%)
  matrix products  83.8 us (21%)
  between operations  14.5 us (4%)
  other arithmetic  8.13 us (2%)
  local copies, waits for them, and re-layouts  7.38 us (2%)
  blocking collectives  7.09 us (2%)
    reduce_scatter x2, waiting for transfers between devices, collect(): lax.psum_scatter(term_fn(jnp.int32(0), lax.axis_size('dp') * count), 'dp'...  123 us
    all_gather x2, waiting for transfers between devices, spread(): return lax.all_gather(block, 'dp', axis=0, tiled=True)  66.5 us
    psum x1, waiting for transfers between devices, on_device(): gain_grad = lax.psum(gain_part, 'dp')  64.9 us
    dot_general x2, matrix products, contract_last(): lax.dot_general(left, right, (((1,), (1,)), ((), ())), preferred_element_...  24.2 us
    dot_general x2, matrix products, contract_first(): lax.dot_general(left, right, (((0,), (0,)), ((), ())), preferred_element_...  22.4 us
    psum x1, waiting for transfers between devices, over_slots(): return lax.psum(partial_rows, 'sect')  14.2 us
    dot_general x1, matrix products, output_term(): return jnp.dot(activated, down_local, preferred_element_type=jnp.float32)  12.9 us
    dot_general x1, matrix products, norm_term(): return jnp.dot(pre_grad, up_local, preferred_element_type=jnp.float32)  12.9 us
  transfers between devices with their start and end apart: 6, of which 6 were waited for; matrix products, arithmetic and copies ran while one was open for 15% of the time, Pallas kernels for 0%

commit v1 on v0

v1 whole, which is shorter than its diff:
```python
import functools

import jax
import jax.numpy as jnp
from jax import lax
from jax.experimental import pallas as pl
from jax.experimental.pallas import tpu as pltpu
from jax.sharding import PartitionSpec as P

HD = 128
MODALITIES = 3


def causal_forward(queries, keys, values):
    seq_count, length, width = queries.shape
    head_count = width // HD
    query_f = queries.astype(jnp.float32).reshape(seq_count, length, head_count, HD)
    key_f = keys.astype(jnp.float32).reshape(seq_count, length, head_count, HD)
    value_f = values.astype(jnp.float32).reshape(seq_count, length, head_count, HD)
    scores = jnp.einsum("sqhd,skhd->shqk", query_f, key_f) * HD ** (-0.5)
    position = jnp.arange(length)
    causal = position[:, None] >= position[None, :]
    scores = jnp.where(causal, scores, -1e30)
    probs = jax.nn.softmax(scores, axis=-1)
    probs_b = probs.astype(jnp.bfloat16)
    attended = jnp.einsum("shqk,skhd->sqhd", probs_b.astype(jnp.float32), value_f)
    return (attended.astype(jnp.bfloat16).reshape(seq_count, length, width), probs, probs_b)


def causal_backward(grad_out, queries, keys, values, attended, probs, probs_b):
    seq_count, length, width = queries.shape
    head_count = width // HD
    shape = (seq_count, length, head_count, HD)
    grad_f = grad_out.astype(jnp.float32).reshape(shape)
    query_f = queries.astype(jnp.float32).reshape(shape)
    key_f = keys.astype(jnp.float32).reshape(shape)
    value_f = values.astype(jnp.float32).reshape(shape)
    attended_f = attended.astype(jnp.float32).reshape(shape)
    value_grad = jnp.einsum("shqk,sqhd->skhd", probs_b.astype(jnp.float32), grad_f).astype(
        jnp.bfloat16
    )
    dprob = jnp.einsum("sqhd,skhd->shqk", grad_f, value_f)
    delta = jnp.einsum("sqhd,sqhd->shq", grad_f, attended_f)
    dscore = (
        (probs * (dprob - delta[..., None]) * HD ** (-0.5)).astype(jnp.bfloat16).astype(jnp.float32)
    )
    query_grad = jnp.einsum("shqk,skhd->sqhd", dscore, key_f).astype(jnp.bfloat16)
    key_grad = jnp.einsum("shqk,sqhd->skhd", dscore, query_f).astype(jnp.bfloat16)
    return (
        query_grad.reshape(seq_count, length, width),
        key_grad.reshape(seq_count, length, width),
        value_grad.reshape(seq_count, length, width),
    )


MESH = pl.DeviceIdType.MESH
VMEM_BYTES = 60 * 1024 * 1024


def remote(src, dst, send_sem, recv_sem, dp_index, sect_index):
    return pltpu.make_async_remote_copy(
        src_ref=src,
        dst_ref=dst,
        send_sem=send_sem,
        recv_sem=recv_sem,
        device_id=(dp_index, sect_index),
        device_id_type=MESH,
    )


def greet(peers):
    barrier = pltpu.get_barrier_semaphore()
    total = jnp.int32(0)
    for dp_index, sect_index, present in peers:
        if present is None:
            pl.semaphore_signal(barrier, inc=1, device_id=(dp_index, sect_index), device_id_type=MESH)
            total = total + 1
        else:

            @pl.when(present)
            def _():
                pl.semaphore_signal(
                    barrier, inc=1, device_id=(dp_index, sect_index), device_id_type=MESH
                )

            total = total + present.astype(jnp.int32)
    pl.semaphore_wait(barrier, total)


class LineGather:
    def __init__(self, buf, sems, lines, slot):
        self.buf, self.lines = buf, lines
        self.send_sems, self.recv_sems = sems
        self.slot = slot
        self.me = lax.axis_index("dp")
        self.sect = lax.axis_index("sect")
        self.outer, self.inner = self.me // 2, self.me % 2

    def copy(self, way, outer, target, incoming=False):
        inner = (1 - self.inner) if (incoming and way == 2) else self.inner
        block = self.buf.at[outer * 2 + inner]
        recv = 1 if way == 2 else 0
        return remote(
            block,
            block,
            self.send_sems.at[self.slot, way, outer],
            self.recv_sems.at[self.slot, recv, outer],
            target,
            self.sect,
        )

    def pass_up(self, outer):
        return self.copy(0, outer, jnp.minimum(self.outer + 1, self.lines - 1) * 2 + self.inner)

    def pass_down(self, outer):
        return self.copy(1, outer, jnp.maximum(self.outer - 1, 0) * 2 + self.inner)

    def pass_across(self, outer):
        return self.copy(2, outer, self.outer * 2 + 1 - self.inner)

    def start(self):
        outer = self.outer

        @pl.when(outer + 1 < self.lines)
        def _():
            self.pass_up(outer).start()

        @pl.when(outer > 0)
        def _():
            self.pass_down(outer).start()

        self.pass_across(outer).start()

    def relay(self, step):
        outer = self.outer

        @pl.when(outer - step >= 0)
        def _():
            block = outer - step
            self.pass_down(block).wait_recv()

            @pl.when(outer + 1 < self.lines)
            def _():
                self.pass_up(block).start()

            self.pass_across(block).start()

        @pl.when(outer + step < self.lines)
        def _():
            block = outer + step
            self.pass_up(block).wait_recv()

            @pl.when(outer > 0)
            def _():
                self.pass_down(block).start()

            self.pass_across(block).start()

    def finish(self):
        outer = self.outer
        for block in range(self.lines):
            self.copy(2, block, self.outer * 2 + 1 - self.inner, incoming=True).wait_recv()
            self.pass_across(block).wait_send()

            @pl.when((outer + 1 < self.lines) & (block <= outer))
            def _():
                self.pass_up(block).wait_send()

            @pl.when((outer > 0) & (block >= outer))
            def _():
                self.pass_down(block).wait_send()


def front_kernel(
    lines, slots, att_ref, res_ref, gain_ref, sel_ref, cot_ref, hidden_ref, norm_ref, rows_ref, cots_ref,
    att_all, send_sems, recv_sems, att_send, att_recv,
):
    me, sect = lax.axis_index("dp"), lax.axis_index("sect")
    outer, inner = me // 2, me % 2
    width = att_ref.shape[1]
    peers = [(me, lax.rem(sect + k, slots), None) for k in range(1, slots)]
    peers.append((outer * 2 + 1 - inner, sect, None))
    peers.append((jnp.minimum(outer + 1, lines - 1) * 2 + inner, sect, outer + 1 < lines))
    peers.append((jnp.maximum(outer - 1, 0) * 2 + inner, sect, outer > 0))
    sel = sel_ref[...]
    cots_ref[me] = jnp.dot(sel, cot_ref[...], preferred_element_type=jnp.float32).astype(jnp.bfloat16)
    greet(peers)
    copies = []
    for k in range(1, slots):
        target = lax.rem(sect + k, slots)
        copies.append(
            remote(att_ref, att_all.at[sect], att_send.at[k], att_recv.at[sect], me, target)
        )
        copies[-1].start()
    cots = LineGather(cots_ref, (send_sems, recv_sems), lines, 0)
    rows = LineGather(rows_ref, (send_sems, recv_sems), lines, 1)
    cots.start()
    att_all[sect] = att_ref[...]
    for k in range(1, slots):
        source = lax.rem(sect + k, slots)
        remote(att_ref, att_all.at[source], att_send.at[k], att_recv.at[source], me, source).wait_recv()
    square = jnp.zeros((res_ref.shape[0], 1), jnp.float32)
    for block in range(slots):
        cols = slice(block * width, (block + 1) * width)
        hid = (
            res_ref[:, cols].astype(jnp.float32) + att_all[block].astype(jnp.float32)
        ).astype(jnp.bfloat16)
        hidden_ref[:, cols] = hid
        hid_f = hid.astype(jnp.float32)
        square = square + jnp.sum(hid_f * hid_f, axis=-1, keepdims=True)
    inverse = lax.rsqrt(square / (slots * width) + 1e-05)
    norm_ref[...] = jnp.broadcast_to(inverse, norm_ref.shape)
    for block in range(slots):
        cols = slice(block * width, (block + 1) * width)
        normed = (hidden_ref[:, cols].astype(jnp.float32) * inverse * gain_ref[:, cols]).astype(
            jnp.bfloat16
        )
        rows_ref[me, :, cols] = jnp.dot(sel, normed, preferred_element_type=jnp.float32).astype(
            jnp.bfloat16
        )
    rows.start()
    for step in range(1, lines):
        cots.relay(step)
        rows.relay(step)
    cots.finish()
    rows.finish()
    for one in copies:
        one.wait_send()


def front(att, residual, gain_rows, selector, cotangent, dp, slots):
    length, width = residual.shape
    capacity = selector.shape[0]
    vm = pl.BlockSpec(memory_space=pltpu.VMEM)
    return pl.pallas_call(
        functools.partial(front_kernel, dp // 2, slots),
        out_shape=(
            jax.ShapeDtypeStruct((length, width), jnp.bfloat16),
            jax.ShapeDtypeStruct((length, 128), jnp.float32),
            jax.ShapeDtypeStruct((dp, capacity, width), jnp.bfloat16),
            jax.ShapeDtypeStruct((dp, capacity, width), jnp.bfloat16),
        ),
        in_specs=[vm] * 5,
        out_specs=(vm,) * 4,
        scratch_shapes=[
            pltpu.VMEM((slots,) + att.shape, jnp.bfloat16),
            pltpu.SemaphoreType.DMA((2, 3, dp // 2)),
            pltpu.SemaphoreType.DMA((2, 2, dp // 2)),
            pltpu.SemaphoreType.DMA((slots,)),
            pltpu.SemaphoreType.DMA((slots,)),
        ],
        compiler_params=pltpu.CompilerParams(
            collective_id=0, has_side_effects=True, vmem_limit_bytes=VMEM_BYTES
        ),
    )(att, residual, gain_rows, selector, cotangent)


def ffn_kernel(tail, rows_ref, cots_ref, up_ref, down_ref, out_ref, back_ref, upg_ref, downg_ref, out_acc, back_acc):
    step = pl.program_id(0)
    last = pl.num_programs(0) - 1
    full = up_ref.shape[0]

    @pl.when(step == 0)
    def _():
        out_acc[...] = jnp.zeros_like(out_acc)
        back_acc[...] = jnp.zeros_like(back_acc)

    def run(size):
        rows, cots = rows_ref[...], cots_ref[...]
        preact = contract_last(rows, up_ref[:size, :])
        back = contract_last(cots, down_ref[:size, :])
        sigma = jax.nn.sigmoid(preact)
        activated = (preact * sigma).astype(jnp.bfloat16)
        pre_grad = (back * sigma * (1.0 + preact * (1.0 - sigma))).astype(jnp.bfloat16)
        out_acc[...] += jnp.dot(activated, down_ref[:size, :], preferred_element_type=jnp.float32)
        back_acc[...] += jnp.dot(pre_grad, up_ref[:size, :], preferred_element_type=jnp.float32)
        downg_ref[:size, :] = contract_first(activated, cots).astype(jnp.bfloat16)
        upg_ref[:size, :] = contract_first(pre_grad, rows).astype(jnp.bfloat16)

    if tail == full:
        run(full)
    else:

        @pl.when(step < last)
        def _():
            run(full)

        @pl.when(step == last)
        def _():
            run(tail)

    @pl.when(step == last)
    def _():
        out_ref[...] = out_acc[...].astype(jnp.bfloat16)
        back_ref[...] = back_acc[...].astype(jnp.bfloat16)


def ffn(rows, cots, up, down):
    count, width = rows.shape
    hidden_units = up.shape[0]
    chunk = min(256 if count <= 128 else 128, hidden_units)
    steps = pl.cdiv(hidden_units, chunk)
    tail = hidden_units - (steps - 1) * chunk
    whole = pl.BlockSpec((count, width), lambda i: (0, 0))
    weight = pl.BlockSpec((chunk, width), lambda i: (i, 0))
    return pl.pallas_call(
        functools.partial(ffn_kernel, tail),
        grid=(steps,),
        out_shape=(
            jax.ShapeDtypeStruct((count, width), jnp.bfloat16),
            jax.ShapeDtypeStruct((count, width), jnp.bfloat16),
            jax.ShapeDtypeStruct(up.shape, jnp.bfloat16),
            jax.ShapeDtypeStruct(down.shape, jnp.bfloat16),
        ),
        in_specs=[whole, whole, weight, weight],
        out_specs=(whole, whole, weight, weight),
        scratch_shapes=[
            pltpu.VMEM((count, width), jnp.float32),
            pltpu.VMEM((count, width), jnp.float32),
        ],
        compiler_params=pltpu.CompilerParams(
            dimension_semantics=("arbitrary",), vmem_limit_bytes=VMEM_BYTES
        ),
    )(rows, cots, up, down)


def reduce_kernel(lines, slots, out_in, back_in, sums_ref, from_pair, pair_sum, from_line, pair_send, pair_recv,
                  line_send, line_recv, sect_send, sect_recv):
    me, sect = lax.axis_index("dp"), lax.axis_index("sect")
    outer, inner = me // 2, me % 2
    partner = outer * 2 + 1 - inner
    terms = (back_in, out_in)
    peers = [(me, lax.rem(sect + k, slots), None) for k in range(1, slots)]
    peers.append((partner, sect, None))
    for k in range(1, lines):
        peers.append((lax.rem(outer + k, lines) * 2 + inner, sect, None))
    greet(peers)
    order = [(k, step) for k in range(2) for step in list(range(1, lines)) + [0]]

    def across(k, step):
        line = lax.rem(outer + step, lines)
        return remote(
            terms[k].at[line * 2 + 1 - inner],
            from_pair.at[k, step],
            pair_send.at[k, step],
            pair_recv.at[k, step],
            partner,
            sect,
        )

    def along(k, step):
        line = lax.rem(outer + step, lines)
        return remote(
            pair_sum.at[k, step],
            from_line.at[k, step],
            line_send.at[k, step],
            line_recv.at[k, step],
            line * 2 + inner,
            sect,
        )

    def to_sect(k, hop):
        target = lax.rem(sect + hop, slots)
        return remote(
            sums_ref.at[k, sect],
            sums_ref.at[k, sect],
            sect_send.at[k, hop],
            sect_recv.at[k, sect],
            me,
            target,
        )

    def from_sect(k, hop):
        source = lax.rem(sect + hop, slots)
        return remote(
            sums_ref.at[k, source],
            sums_ref.at[k, source],
            sect_send.at[k, hop],
            sect_recv.at[k, source],
            me,
            source,
        )

    for k, step in order:
        across(k, step).start()
    for k in range(2):
        for step in list(range(1, lines)) + [0]:
            across(k, step).wait_recv()
            line = lax.rem(outer + step, lines)
            own = terms[k][line * 2 + inner].astype(jnp.float32) + from_pair[k, step].astype(jnp.float32)
            if step:
                pair_sum[k, step] = own.astype(jnp.bfloat16)
                along(k, step).start()
        for step in range(1, lines):
            along(k, step).wait_recv()
            own = own + from_line[k, step].astype(jnp.float32)
        sums_ref[k, sect] = own.astype(jnp.bfloat16)
        for hop in range(1, slots):
            to_sect(k, hop).start()
    for k in range(2):
        for hop in range(1, slots):
            from_sect(k, hop).wait_recv()
            to_sect(k, hop).wait_send()
        for step in range(lines):
            across(k, step).wait_send()
            if step:
                along(k, step).wait_send()


def reduce_terms(out_terms, back_terms, slots):
    dp, capacity, width = out_terms.shape
    lines = dp // 2
    vm = pl.BlockSpec(memory_space=pltpu.VMEM)
    dma = pltpu.SemaphoreType.DMA
    return pl.pallas_call(
        functools.partial(reduce_kernel, lines, slots),
        out_shape=jax.ShapeDtypeStruct((2, slots, capacity, width), jnp.bfloat16),
        in_specs=[vm] * 2,
        out_specs=vm,
        scratch_shapes=[
            pltpu.VMEM((2, lines, capacity, width), jnp.bfloat16),
            pltpu.VMEM((2, lines, capacity, width), jnp.bfloat16),
            pltpu.VMEM((2, lines, capacity, width), jnp.bfloat16),
            dma((2, lines)),
            dma((2, lines)),
            dma((2, lines)),
            dma((2, lines)),
            dma((2, slots)),
            dma((2, slots)),
        ],
        compiler_params=pltpu.CompilerParams(
            collective_id=1, has_side_effects=True, vmem_limit_bytes=VMEM_BYTES
        ),
    )(out_terms, back_terms)


def gain_kernel(dp, slots, part_ref, total_ref, inbox, mine, first_send, first_recv, next_send, next_recv, sect_send, sect_recv):
    me, sect = lax.axis_index("dp"), lax.axis_index("sect")
    peers = [(me, lax.rem(sect + k, slots), None) for k in range(1, slots)]
    peers += [(lax.rem(me + k, dp), sect, None) for k in range(1, dp)]
    greet(peers)

    def scatter(k):
        target = lax.rem(me + k, dp)
        return remote(
            part_ref.at[sect, target], inbox.at[k], first_send.at[k], first_recv.at[k], target, sect
        )

    def spread_sum(k):
        target = lax.rem(me + k, dp)
        return remote(
            mine, total_ref.at[sect, me], next_send.at[k], next_recv.at[k], target, sect
        )

    def to_sect(k):
        return remote(
            total_ref.at[sect],
            total_ref.at[sect],
            sect_send.at[k],
            sect_recv.at[k],
            me,
            lax.rem(sect + k, slots),
        )

    for k in range(1, dp):
        scatter(k).start()
    total = part_ref[sect, me]
    for k in range(1, dp):
        scatter(k).wait_recv()
        total = total + inbox[k]
    mine[...] = total
    for k in range(1, dp):
        spread_sum(k).start()
    total_ref[sect, me] = total
    for k in range(1, dp):
        spread_sum(k).wait_recv()
    for k in range(1, slots):
        to_sect(k).start()
    for k in range(1, slots):
        to_sect(k).wait_recv()
        to_sect(k).wait_send()
    for k in range(1, dp):
        scatter(k).wait_send()
        spread_sum(k).wait_send()


def gain_sum(part, dp, slots):
    kinds, width = part.shape
    cols = width // (dp * slots)
    padded = jnp.concatenate([part, jnp.zeros((8 - kinds, width), part.dtype)], 0)
    pieces = padded.reshape(8, slots, dp, cols).transpose(1, 2, 0, 3)
    vm = pl.BlockSpec(memory_space=pltpu.VMEM)
    dma = pltpu.SemaphoreType.DMA
    total = pl.pallas_call(
        functools.partial(gain_kernel, dp, slots),
        out_shape=jax.ShapeDtypeStruct(pieces.shape, pieces.dtype),
        in_specs=[vm],
        out_specs=vm,
        scratch_shapes=[
            pltpu.VMEM((dp, 8, cols), pieces.dtype),
            pltpu.VMEM((8, cols), pieces.dtype),
            dma((dp,)),
            dma((dp,)),
            dma((dp,)),
            dma((dp,)),
            dma((slots,)),
            dma((slots,)),
        ],
        compiler_params=pltpu.CompilerParams(collective_id=2, has_side_effects=True),
    )(pieces)
    return total.transpose(2, 0, 1, 3).reshape(8, width)[:kinds]


def contract_last(left, right):
    return lax.dot_general(
        left, right, (((1,), (1,)), ((), ())), preferred_element_type=jnp.float32
    )


def contract_first(left, right):
    return lax.dot_general(
        left, right, (((0,), (0,)), ((), ())), preferred_element_type=jnp.float32
    )


def selectors(token_labels, slot_modality):
    length = token_labels.shape[0]
    keep = token_labels[None, :] == slot_modality[:, None]
    rank = jnp.cumsum(keep.astype(jnp.int32), axis=1) - 1
    capacity = length // 2
    return (rank[:, None, :] == jnp.arange(capacity)[None, :, None]) & keep[:, None, :]


def on_device(
    dp, slots, queries, keys, values, residual, labels, slot_modality, gains, up_weight, down_weight, cotangent
):
    attended_block, probs, probs_b = causal_forward(queries, keys, values)
    token_labels = labels[0]
    onehot = (token_labels[:, None] == jnp.arange(MODALITIES)[None, :]).astype(jnp.float32)
    gain_rows = jnp.dot(onehot, gains, precision=lax.Precision.HIGHEST)
    slot_index = lax.axis_index("sect")
    all_select = selectors(token_labels, slot_modality).astype(jnp.bfloat16)
    selector = lax.dynamic_index_in_dim(all_select, slot_index, 0, keepdims=False)
    capacity, length = selector.shape
    grad_full = cotangent[0]
    hidden, inverse, rows, cots = front(
        attended_block[0], residual[0], gain_rows, selector, grad_full, dp, slots
    )
    width = hidden.shape[1]
    inverse = inverse[:, :1]
    hidden_f = hidden.astype(jnp.float32)
    normed_f = hidden_f * inverse
    out_terms, back_terms, up_grad, down_grad = ffn(
        rows.reshape(-1, width), cots.reshape(-1, width), up_weight[0], down_weight[0]
    )
    sums = reduce_terms(
        out_terms.reshape(dp, capacity, width), back_terms.reshape(dp, capacity, width), slots
    ).reshape(2, slots * capacity, width)
    place = all_select.reshape(slots * capacity, length)
    norm_grad = contract_first(place, sums[0])
    quarter = length // slots
    place_own = lax.dynamic_slice_in_dim(place, slot_index * quarter, quarter, 1)
    hidden_own = lax.dynamic_slice_in_dim(hidden_f, slot_index * quarter, quarter, 0)
    output = (hidden_own + contract_first(place_own, sums[1])).astype(jnp.bfloat16)[None]
    scaled = norm_grad * gain_rows
    hidden_grad = grad_full.astype(jnp.float32) + inverse * (
        scaled - normed_f * jnp.mean(scaled * normed_f, axis=-1, keepdims=True)
    )
    residual_full = hidden_grad.astype(jnp.bfloat16)
    residual_grad = lax.dynamic_slice_in_dim(residual_full, slot_index * quarter, quarter, 0)[None]
    gain_part = jnp.dot(onehot.T, norm_grad * normed_f, precision=lax.Precision.HIGHEST)
    gain_grad = gain_sum(gain_part, dp, slots)
    block_width = queries.shape[2]
    grad_block = lax.dynamic_slice_in_dim(residual_full, slot_index * block_width, block_width, 1)[
        None
    ]
    query_grad, key_grad, value_grad = causal_backward(
        grad_block, queries, keys, values, attended_block, probs, probs_b
    )
    return (
        output, residual_grad, query_grad, key_grad, value_grad, up_grad[None], down_grad[None], gain_grad,
    )


def solution(mesh):
    in_specs = (
        P("dp", None, "sect"),
        P("dp", None, "sect"),
        P("dp", None, "sect"),
        P("dp", None, None),
        P("dp", None),
        P(),
        P(),
        P("sect", "dp", None),
        P("sect", "dp", None),
        P("dp", None, None),
    )
    out_specs = (
        P("dp", "sect", None),
        P("dp", "sect", None),
        P("dp", None, "sect"),
        P("dp", None, "sect"),
        P("dp", None, "sect"),
        P("sect", "dp", None),
        P("sect", "dp", None),
        P(),
    )
    body = functools.partial(on_device, mesh.shape["dp"], mesh.shape["sect"])
    return jax.shard_map(
        body, mesh=mesh, in_specs=in_specs, out_specs=out_specs, check_vma=False
    )
```

time: 393 us -> 152 us (0.39)
  waiting for transfers between devices: 269 us -> 0 us
  Pallas kernels: 0 us -> 134 us
  matrix products: 83.8 us -> 6.84 us
  between operations: 14.5 us -> 0.85 us
  blocking collectives: 7.09 us -> 0 us
  other arithmetic: 8.13 us -> 1.96 us
    pallas_call x0 -> x4, Pallas kernels: none -> 134 us  [the longest x1 41.6 us: ffn(): pl.pallas_call(functools.partial(ffn_kernel, tail), grid=(steps,), out_sh...]
    reduce_scatter x2 -> x0, waiting for transfers between devices: 123 us -> none  [collect(): lax.psum_scatter(term_fn(jnp.int32(0), lax.axis_size('dp') * count), 'dp'...]
    psum x2 -> x0, waiting for transfers between devices: 79.1 us -> none  [the longest x1 64.9 us: on_device(): gain_grad = lax.psum(gain_part, 'dp')]
    all_gather x2 -> x0, waiting for transfers between devices: 66.5 us -> none  [spread(): return lax.all_gather(block, 'dp', axis=0, tiled=True)]
    dot_general x8 -> x0, matrix products: 57 us -> none  [the longest x2 24.2 us: contract_last(): lax.dot_general(left, right, (((1,), (1,)), ((), ())), preferred_element_...]
    dot_general x2, matrix products: 22.4 us -> 3.44 us  [contract_first(): lax.dot_general(left, right, (((0,), (0,)), ((), ())), preferred_element_...]
    all_gather x1 -> x0, blocking collectives: 7.09 us -> none  [on_device(): attended = lax.all_gather(attended_block, 'sect', axis=2, tiled=True)]
  transfers between devices with their start and end apart: 6 -> 0, of which waited for: 6 -> 0; matrix products, arithmetic and copies ran while one was open for 15% -> 0% of each run, Pallas kernels for 0% -> 0%
where the time goes in v1:
time: 152 us
  Pallas kernels  134 us (88%)
  local copies, waits for them, and re-layouts  7.84 us (5%)
  matrix products  6.84 us (4%)
  other arithmetic  1.96 us (1%)
    pallas_call x1, Pallas kernels, ffn(): pl.pallas_call(functools.partial(ffn_kernel, tail), grid=(steps,), out_sh...  41.6 us
    pallas_call x1, Pallas kernels, reduce_terms(): pl.pallas_call(functools.partial(reduce_kernel, lines, slots), out_shape=...  40.6 us
    pallas_call x1, Pallas kernels, front(): pl.pallas_call(functools.partial(front_kernel, dp // 2, slots), out_shape...  32.7 us
    pallas_call x1, Pallas kernels, gain_sum(): pl.pallas_call(functools.partial(gain_kernel, dp, slots), out_shape=jax.S...  19.4 us
    dot_general x2, matrix products, contract_first(): lax.dot_general(left, right, (((0,), (0,)), ((), ())), preferred_element_...  3.44 us
    unnamed x18, local copies, waits for them, and re-layouts  3.27 us

profile of v1, /device:TPU:1, one launch (start us, length us, event | category | flops | bytes accessed | tf_op | source)
XLA Modules:
  0.0 151.8 jit_solution(5091304724987147322)
XLA Ops:
  0.6 0.0 copy-start
  0.7 0.8 fusion.47
  1.4 0.2 reduce_window_sum.11
  1.6 0.6 fusion.42.sel_ref
  2.2 0.8 copy.56
  3.1 0.9 copy.57
  4.0 0.2 fusion.48
  4.2 0.9 copy.58
  5.0 0.2 convolution_convert_fusion.3
  5.3 0.6 copy.90
  5.9 1.9 %fusion.39.gain_ref = f32[16,8192]{1,0:T(8,128)} fusion(f32[3,8192]{1,0:T(4,128)S(1)} %copy-done, s32[16]{0:T(128)} %bitcast.130), kind=kOutput, calls=%fused_computation.62 | convolution fusion | flops 4718640 | bytes 622656 | tf_op jit(solution)/shard_map/dot_general | solution.py:540
  7.8 32.7 %shard_map.161 = (bf16[16,8192]{1,0:T(8,128)(2,1)}, f32[16,128]{1,0:T(8,128)}, bf16[8,8,8192]{2,1,0:T(8,128)(2,1)}, bf16[8,8,8192]{2,1,0:T(8,128)(2,1)}) custom-call(bf16[16,2048]{1,0:T(8,128)(2,1)} %bitcast.120, bf16[16,8192]{1,0:T(8,128)(2,1)} %bitcast.114, f32[16,8192]{1,0:T(8,128)} %fusion.39.gain_ref, bf16[8,16]{1,0:T(8,128)(2,1)} %fusion.42.sel_ref, ...), custom_call_target="tpu_custom_call" | custom-call | tf_op jit(solution)/shard_map/pallas_call | solution.py:235
  40.5 0.0 copy-start.3
  40.5 41.6 %shard_map.162 = (bf16[64,8192]{1,0:T(8,128)(2,1)}, bf16[64,8192]{1,0:T(8,128)(2,1)}, bf16[1376,8192]{1,0:T(8,128)(2,1)}, bf16[1376,8192]{1,0:T(8,128)(2,1)}) custom-call(bf16[64,8192]{1,0:T(8,128)(2,1)} %bitcast.107, bf16[64,8192]{1,0:T(8,128)(2,1)} %bitcast.108, bf16[1376,8192]{1,0:T(8,128)(2,1)} %bitcast.105, bf16[1376,8192]{1,0:T(8,128)(2,1)} %bitcast.106), custom_call_target="tpu_custom_call" | custom-call | tf_op jit(solution)/shard_map/pallas_call | solution.py:306
  82.1 40.6 %shard_map.163 = bf16[2,4,8,8192]{3,2,1,0:T(8,128)(2,1)} custom-call(bf16[8,8,8192]{2,1,0:T(8,128)(2,1)} %bitcast.109, bf16[8,8,8192]{2,1,0:T(8,128)(2,1)} %bitcast.110), custom_call_target="tpu_custom_call" | custom-call | tf_op jit(solution)/shard_map/pallas_call | solution.py:415
  122.7 0.1 slice_reduce_fusion
  122.9 1.4 multiply_reduce_fusion
  124.3 0.4 fusion.15
  124.8 0.7 concatenate.3
  125.5 19.4 %shard_map.164 = f32[4,8,8,256]{3,2,1,0:T(8,128)} custom-call(f32[4,8,8,256]{3,2,1,0:T(8,128)} %bitcast.112), custom_call_target="tpu_custom_call" | custom-call | tf_op jit(solution)/shard_map/pallas_call | solution.py:494
  144.9 1.6 %slice.22 = f32[3,4,8,256]{3,0,2,1:T(4,128)} slice(f32[8,4,8,256]{3,0,2,1:T(8,128)} %bitcast.113), slice={[0:3], [0:4], [0:8], [0:256]} | slice | bytes 196608 | tf_op jit(solution)/shard_map/slice | solution.py:511
  146.6 0.2 add_convert_fusion
  146.8 0.2 fusion.11
  147.0 0.1 multiply_reduce_fusion.1
  147.1 0.2 fusion.8
  147.3 0.2 fusion.10
  147.5 0.7 copy_bitcast_fusion.1
  148.1 0.2 fusion.9
  148.3 0.6 copy.91
  149.0 0.7 dynamic-slice_bitcast_fusion
  149.7 0.1 eq.79
  149.8 2.0 %fusion.2 = bf16[1,4,8192]{2,1,0:T(4,128)(2,1)} fusion(bf16[2,4,8,8192]{3,2,1,0:T(8,128)(2,1)} %shard_map.163, f32[16,8192]{1,0:T(8,128)S(1)} %convert_element_type.94, s32[]{:T(128)S(6)} %select_n.19, s32[32,16]{1,0:T(8,128)S(1)} %broadcast_bitcast_fusion, pred[32,16]{1,0:T(32,128)(4,1)S(1)} %get-tuple-element.30, s32[32]{0:T(128)S(1)} %eq.79), kind=kOutput, calls=%fused_computation.3 | convolution fusion | flops 2162944 | bytes 724608 | tf_op jit(solution)/shard_map/dot_general | solution.py:521
  (21 shorter events, 0.2 us)
Async XLA Ops:
  0.6 5.3 %copy-start = (f32[3,8192]{1,0:T(4,128)S(1)}, f32[3,8192]{1,0:T(4,128)}, u32[]{:S(2)}) copy-start(f32[3,8192]{1,0:T(4,128)} %param.16) | copy-start | bytes 294916
  40.5 82.3 %copy-start.4 = (f32[16,128]{1,0:T(8,128)S(1)}, f32[16,128]{1,0:T(8,128)}, u32[]{:S(2)}) copy-start(f32[16,128]{1,0:T(8,128)} %get-tuple-element.21) | copy-start | bytes 24580
  40.5 82.4 %copy-start.1 = (f32[16,8192]{1,0:T(8,128)S(1)}, f32[16,8192]{1,0:T(8,128)}, u32[]{:S(2)}) copy-start(f32[16,8192]{1,0:T(8,128)} %fusion.39.gain_ref) | copy-start | bytes 1572868
  40.5 82.4 %copy-start.2 = (bf16[16,8192]{1,0:T(8,128)(2,1)S(1)}, bf16[16,8192]{1,0:T(8,128)(2,1)}, u32[]{:S(2)}) copy-start(bf16[16,8192]{1,0:T(8,128)(2,1)} %get-tuple-element.16) | copy-start | bytes 786436
  40.5 83.8 %copy-start.5 = (s32[1,16]{1,0:T(1,128)S(1)}, s32[1,16]{1,0:T(1,128)}, u32[]{:S(2)}) copy-start(s32[1,16]{1,0:T(1,128)} %param.14) | copy-start | bytes 196
  40.5 106.1 %copy-start.3 = (bf16[1,16,8192]{2,1,0:T(8,128)(2,1)S(1)}, bf16[1,16,8192]{2,1,0:T(8,128)(2,1)}, u32[]{:S(2)}) copy-start(bf16[1,16,8192]{2,1,0:T(8,128)(2,1)} %param.19) | copy-start | bytes 786436

commit v2 on v1

--- a/solution.py
+++ b/solution.py
@@ -25,32 +25,6 @@
     probs_b = probs.astype(jnp.bfloat16)
     attended = jnp.einsum("shqk,skhd->sqhd", probs_b.astype(jnp.float32), value_f)
     return (attended.astype(jnp.bfloat16).reshape(seq_count, length, width), probs, probs_b)
-
-
-def causal_backward(grad_out, queries, keys, values, attended, probs, probs_b):
-    seq_count, length, width = queries.shape
-    head_count = width // HD
-    shape = (seq_count, length, head_count, HD)
-    grad_f = grad_out.astype(jnp.float32).reshape(shape)
-    query_f = queries.astype(jnp.float32).reshape(shape)
-    key_f = keys.astype(jnp.float32).reshape(shape)
-    value_f = values.astype(jnp.float32).reshape(shape)
-    attended_f = attended.astype(jnp.float32).reshape(shape)
-    value_grad = jnp.einsum("shqk,sqhd->skhd", probs_b.astype(jnp.float32), grad_f).astype(
-        jnp.bfloat16
-    )
-    dprob = jnp.einsum("sqhd,skhd->shqk", grad_f, value_f)
-    delta = jnp.einsum("sqhd,sqhd->shq", grad_f, attended_f)
-    dscore = (
-        (probs * (dprob - delta[..., None]) * HD ** (-0.5)).astype(jnp.bfloat16).astype(jnp.float32)
-    )
-    query_grad = jnp.einsum("shqk,skhd->sqhd", dscore, key_f).astype(jnp.bfloat16)
-    key_grad = jnp.einsum("shqk,sqhd->skhd", dscore, query_f).astype(jnp.bfloat16)
-    return (
-        query_grad.reshape(seq_count, length, width),
-        key_grad.reshape(seq_count, length, width),
-        value_grad.reshape(seq_count, length, width),
-    )
 
 
 MESH = pl.DeviceIdType.MESH
@@ -324,7 +298,7 @@
     )(rows, cots, up, down)
 
 
-def reduce_kernel(lines, slots, out_in, back_in, sums_ref, from_pair, pair_sum, from_line, pair_send, pair_recv,
+def reduce_kernel(lines, slots, out_in, back_in, norm_sums, out_sums, from_pair, pair_sum, from_line, pair_send, pair_recv,
                   line_send, line_recv, sect_send, sect_recv):
     me, sect = lax.axis_index("dp"), lax.axis_index("sect")
     outer, inner = me // 2, me % 2
@@ -359,26 +333,14 @@
             sect,
         )
 
-    def to_sect(k, hop):
-        target = lax.rem(sect + hop, slots)
+    sums = (norm_sums, out_sums)
+    near = sect + 1 - 2 * (sect % 2)
+    far = lax.rem(sect + 2, slots)
+    far_near = lax.rem(near + 2, slots)
+
+    def hand(k, way, block, target):
         return remote(
-            sums_ref.at[k, sect],
-            sums_ref.at[k, sect],
-            sect_send.at[k, hop],
-            sect_recv.at[k, sect],
-            me,
-            target,
-        )
-
-    def from_sect(k, hop):
-        source = lax.rem(sect + hop, slots)
-        return remote(
-            sums_ref.at[k, source],
-            sums_ref.at[k, source],
-            sect_send.at[k, hop],
-            sect_recv.at[k, source],
-            me,
-            source,
+            sums[k].at[block], sums[k].at[block], sect_send.at[k, way], sect_recv.at[k, block], me, target
         )
 
     for k, step in order:
@@ -394,13 +356,18 @@
         for step in range(1, lines):
             along(k, step).wait_recv()
             own = own + from_line[k, step].astype(jnp.float32)
-        sums_ref[k, sect] = own.astype(jnp.bfloat16)
-        for hop in range(1, slots):
-            to_sect(k, hop).start()
+        sums[k][sect] = own.astype(sums[k].dtype)
+        hand(k, 1, sect, far).start()
+        hand(k, 0, sect, near).start()
     for k in range(2):
-        for hop in range(1, slots):
-            from_sect(k, hop).wait_recv()
-            to_sect(k, hop).wait_send()
+        hand(k, 1, far, far).wait_recv()
+        hand(k, 2, far, near).start()
+    for k in range(2):
+        hand(k, 0, near, near).wait_recv()
+        hand(k, 2, far_near, near).wait_recv()
+        hand(k, 0, sect, near).wait_send()
+        hand(k, 1, sect, far).wait_send()
+        hand(k, 2, far, near).wait_send()
         for step in range(lines):
             across(k, step).wait_send()
             if step:
@@ -414,9 +381,12 @@
     dma = pltpu.SemaphoreType.DMA
     return pl.pallas_call(
         functools.partial(reduce_kernel, lines, slots),
-        out_shape=jax.ShapeDtypeStruct((2, slots, capacity, width), jnp.bfloat16),
+        out_shape=(
+            jax.ShapeDtypeStruct((slots, capacity, width), jnp.float32),
+            jax.ShapeDtypeStruct((slots, capacity, width), jnp.bfloat16),
+        ),
         in_specs=[vm] * 2,
-        out_specs=vm,
+        out_specs=(vm, vm),
         scratch_shapes=[
             pltpu.VMEM((2, lines, capacity, width), jnp.bfloat16),
             pltpu.VMEM((2, lines, capacity, width), jnp.bfloat16),
@@ -425,7 +395,7 @@
             dma((2, lines)),
             dma((2, lines)),
             dma((2, lines)),
-            dma((2, slots)),
+            dma((2, 3)),
             dma((2, slots)),
         ],
         compiler_params=pltpu.CompilerParams(
@@ -434,7 +404,29 @@
     )(out_terms, back_terms)
 
 
-def gain_kernel(dp, slots, part_ref, total_ref, inbox, mine, first_send, first_recv, next_send, next_recv, sect_send, sect_recv):
+def head_grads(refs, heads):
+    query_ref, key_ref, value_ref, att_ref, grad_ref, query_out, key_out, value_out = refs
+    length = query_ref.shape[0]
+    rows = lax.broadcasted_iota(jnp.int32, (length, length), 0)
+    cols = lax.broadcasted_iota(jnp.int32, (length, length), 1)
+    for head in heads:
+        block = slice(head * HD, (head + 1) * HD)
+        query, key, value, grad = (one[:, block] for one in (query_ref, key_ref, value_ref, grad_ref))
+        scores = jnp.where(rows >= cols, contract_last(query, key) * HD ** (-0.5), -1e30)
+        raised = jnp.exp(scores - jnp.max(scores, axis=-1, keepdims=True))
+        probs = raised / jnp.sum(raised, axis=-1, keepdims=True)
+        value_out[:, block] = contract_first(probs.astype(jnp.bfloat16), grad).astype(jnp.bfloat16)
+        delta = jnp.sum(
+            grad.astype(jnp.float32) * att_ref[:, block].astype(jnp.float32), axis=-1, keepdims=True
+        )
+        dscore = (probs * (contract_last(grad, value) - delta) * HD ** (-0.5)).astype(jnp.bfloat16)
+        query_out[:, block] = jnp.dot(dscore, key, preferred_element_type=jnp.float32).astype(
+            jnp.bfloat16
+        )
+        key_out[:, block] = contract_first(dscore, query).astype(jnp.bfloat16)
+
+
+def gain_kernel(dp, slots, part_ref, query_ref, key_ref, value_ref, att_ref, grad_ref, total_ref, query_out, key_out, value_out, inbox, mine, first_send, first_recv, next_send, next_recv, sect_send, sect_recv):
     me, sect = lax.axis_index("dp"), lax.axis_index("sect")
     peers = [(me, lax.rem(sect + k, slots), None) for k in range(1, slots)]
     peers += [(lax.rem(me + k, dp), sect, None) for k in range(1, dp)]
@@ -464,6 +456,9 @@
 
     for k in range(1, dp):
         scatter(k).start()
+    refs = (query_ref, key_ref, value_ref, att_ref, grad_ref, query_out, key_out, value_out)
+    head_count = query_ref.shape[1] // HD
+    head_grads(refs, range(head_count // 2))
     total = part_ref[sect, me]
     for k in range(1, dp):
         scatter(k).wait_recv()
@@ -472,6 +467,7 @@
     for k in range(1, dp):
         spread_sum(k).start()
     total_ref[sect, me] = total
+    head_grads(refs, range(head_count // 2, head_count))
     for k in range(1, dp):
         spread_sum(k).wait_recv()
     for k in range(1, slots):
@@ -484,18 +480,19 @@
         spread_sum(k).wait_send()
 
 
-def gain_sum(part, dp, slots):
+def gain_sum(part, queries, keys, values, attended, grad, dp, slots):
     kinds, width = part.shape
     cols = width // (dp * slots)
     padded = jnp.concatenate([part, jnp.zeros((8 - kinds, width), part.dtype)], 0)
     pieces = padded.reshape(8, slots, dp, cols).transpose(1, 2, 0, 3)
     vm = pl.BlockSpec(memory_space=pltpu.VMEM)
     dma = pltpu.SemaphoreType.DMA
-    total = pl.pallas_call(
+    like = jax.ShapeDtypeStruct(queries.shape, queries.dtype)
+    total, *grads = pl.pallas_call(
         functools.partial(gain_kernel, dp, slots),
-        out_shape=jax.ShapeDtypeStruct(pieces.shape, pieces.dtype),
-        in_specs=[vm],
-        out_specs=vm,
+        out_shape=(jax.ShapeDtypeStruct(pieces.shape, pieces.dtype), like, like, like),
+        in_specs=[vm] * 6,
+        out_specs=(vm,) * 4,
         scratch_shapes=[
             pltpu.VMEM((dp, 8, cols), pieces.dtype),
             pltpu.VMEM((8, cols), pieces.dtype),
@@ -507,8 +504,8 @@
             dma((slots,)),
         ],
         compiler_params=pltpu.CompilerParams(collective_id=2, has_side_effects=True),
-    )(pieces)
-    return total.transpose(2, 0, 1, 3).reshape(8, width)[:kinds]
+    )(pieces, queries, keys, values, attended, grad)
+    return total.transpose(2, 0, 1, 3).reshape(8, width)[:kinds], grads
 
 
 def contract_last(left, right):
@@ -553,15 +550,20 @@
     out_terms, back_terms, up_grad, down_grad = ffn(
         rows.reshape(-1, width), cots.reshape(-1, width), up_weight[0], down_weight[0]
     )
-    sums = reduce_terms(
+    norm_sums, out_sums = reduce_terms(
         out_terms.reshape(dp, capacity, width), back_terms.reshape(dp, capacity, width), slots
-    ).reshape(2, slots * capacity, width)
+    )
     place = all_select.reshape(slots * capacity, length)
-    norm_grad = contract_first(place, sums[0])
+    norm_grad = lax.dot_general(
+        place.astype(jnp.float32),
+        norm_sums.reshape(slots * capacity, width),
+        (((0,), (0,)), ((), ())),
+        precision=lax.Precision.HIGHEST,
+    )
     quarter = length // slots
     place_own = lax.dynamic_slice_in_dim(place, slot_index * quarter, quarter, 1)
     hidden_own = lax.dynamic_slice_in_dim(hidden_f, slot_index * quarter, quarter, 0)
-    output = (hidden_own + contract_first(place_own, sums[1])).astype(jnp.bfloat16)[None]
+    output = (hidden_own + contract_first(place_own, out_sums.reshape(slots * capacity, width))).astype(jnp.bfloat16)[None]
     scaled = norm_grad * gain_rows
     hidden_grad = grad_full.astype(jnp.float32) + inverse * (
         scaled - normed_f * jnp.mean(scaled * normed_f, axis=-1, keepdims=True)
@@ -569,16 +571,13 @@
     residual_full = hidden_grad.astype(jnp.bfloat16)
     residual_grad = lax.dynamic_slice_in_dim(residual_full, slot_index * quarter, quarter, 0)[None]
     gain_part = jnp.dot(onehot.T, norm_grad * normed_f, precision=lax.Precision.HIGHEST)
-    gain_grad = gain_sum(gain_part, dp, slots)
     block_width = queries.shape[2]
-    grad_block = lax.dynamic_slice_in_dim(residual_full, slot_index * block_width, block_width, 1)[
-        None
-    ]
-    query_grad, key_grad, value_grad = causal_backward(
-        grad_block, queries, keys, values, attended_block, probs, probs_b
+    grad_block = lax.dynamic_slice_in_dim(residual_full, slot_index * block_width, block_width, 1)
+    gain_grad, (query_grad, key_grad, value_grad) = gain_sum(
+        gain_part, queries[0], keys[0], values[0], attended_block[0], grad_block, dp, slots
     )
     return (
-        output, residual_grad, query_grad, key_grad, value_grad, up_grad[None], down_grad[None], gain_grad,
+        output, residual_grad, query_grad[None], key_grad[None], value_grad[None], up_grad[None], down_grad[None], gain_grad,
     )
 
 

time: 152 us -> 156 us (1.026)
  local copies, waits for them, and re-layouts: 7.84 us -> 11.5 us
    unnamed x18 -> x19, local copies, waits for them, and re-layouts: 3.27 us -> 7.65 us
    dot_general x2 -> x1, matrix products: 3.44 us -> 2 us  [contract_first(): lax.dot_general(left, right, (((0,), (0,)), ((), ())), preferred_element_...]
where the time goes in v2:
time: 156 us; the launch traced here: 155 us
  Pallas kernels  134 us (86%)
  local copies, waits for them, and re-layouts  11.5 us (7%)
  matrix products  6.6 us (4%)
  other arithmetic  1.82 us (1%)
    pallas_call x1, Pallas kernels, ffn(): pl.pallas_call(functools.partial(ffn_kernel, tail), grid=(steps,), out_sh...  41.6 us
    pallas_call x1, Pallas kernels, reduce_terms(): pl.pallas_call(functools.partial(reduce_kernel, lines, slots), out_shape=...  39.9 us
    pallas_call x1, Pallas kernels, front(): pl.pallas_call(functools.partial(front_kernel, dp // 2, slots), out_shape...  32.7 us
    pallas_call x1, Pallas kernels, gain_sum(): pl.pallas_call(functools.partial(gain_kernel, dp, slots), out_shape=(jax....  20.1 us
    unnamed x19, local copies, waits for them, and re-layouts  7.65 us

profile of v2, /device:TPU:1, one launch (start us, length us, event | category | flops | bytes accessed | tf_op | source)
XLA Modules:
  0.0 155.0 jit_solution(3956777433154334943)
XLA Ops:
  0.6 0.0 copy-start
  0.7 0.8 fusion.28
  1.4 0.2 reduce_window_sum.11
  1.6 0.6 fusion.25.sel_ref
  2.2 0.8 copy.29
  3.1 0.9 copy.30
  4.0 0.2 fusion.29
  4.2 0.9 copy.31
  5.0 0.2 fusion.6
  5.3 0.6 copy.44
  5.9 0.0 copy-done
  5.9 1.9 %fusion.22.gain_ref = f32[16,8192]{1,0:T(8,128)} fusion(f32[3,8192]{1,0:T(4,128)S(1)} %copy-done, s32[16]{0:T(128)} %bitcast.87), kind=kOutput, calls=%fused_computation.35 | convolution fusion | flops 4718640 | bytes 622656 | tf_op jit(solution)/shard_map/dot_general | solution.py:537
  7.8 32.7 %shard_map.161 = (bf16[16,8192]{1,0:T(8,128)(2,1)}, f32[16,128]{1,0:T(8,128)}, bf16[8,8,8192]{2,1,0:T(8,128)(2,1)}, bf16[8,8,8192]{2,1,0:T(8,128)(2,1)}) custom-call(bf16[16,2048]{1,0:T(8,128)(2,1)} %bitcast.68, bf16[16,8192]{1,0:T(8,128)(2,1)} %bitcast.70, f32[16,8192]{1,0:T(8,128)} %fusion.22.gain_ref, bf16[8,16]{1,0:T(8,128)(2,1)} %fusion.25.sel_ref, ...), custom_call_target="tpu_custom_call" | custom-call | tf_op jit(solution)/shard_map/pallas_call | solution.py:209
  40.5 0.0 copy-start.5
  40.5 0.0 copy-start.3
  40.5 41.6 %shard_map.162 = (bf16[64,8192]{1,0:T(8,128)(2,1)}, bf16[64,8192]{1,0:T(8,128)(2,1)}, bf16[1376,8192]{1,0:T(8,128)(2,1)}, bf16[1376,8192]{1,0:T(8,128)(2,1)}) custom-call(bf16[64,8192]{1,0:T(8,128)(2,1)} %bitcast.62, bf16[64,8192]{1,0:T(8,128)(2,1)} %bitcast.63, bf16[1376,8192]{1,0:T(8,128)(2,1)} %bitcast.60, bf16[1376,8192]{1,0:T(8,128)(2,1)} %bitcast.61), custom_call_target="tpu_custom_call" | custom-call | tf_op jit(solution)/shard_map/pallas_call | solution.py:280
  82.1 39.9 %shard_map.163 = (f32[4,8,8192]{2,1,0:T(8,128)}, bf16[4,8,8192]{2,1,0:T(8,128)(2,1)}) custom-call(bf16[8,8,8192]{2,1,0:T(8,128)(2,1)} %bitcast.64, bf16[8,8,8192]{2,1,0:T(8,128)(2,1)} %bitcast.65), custom_call_target="tpu_custom_call" | custom-call | tf_op jit(solution)/shard_map/pallas_call | solution.py:382
  122.0 0.1 slice_reduce_fusion
  122.1 0.0 copy-done.2
  122.2 1.9 %multiply_reduce_fusion = (f32[16]{0:T(128)S(1)}, f32[16,8192]{1,0:T(8,128)S(1)}, f32[16,8192]{1,0:T(8,128)S(1)}) fusion(bf16[16,8192]{1,0:T(8,128)(2,1)S(1)} %copy-done.2, f32[16]{0:T(128)S(1)} %slice_reduce_fusion, f32[16,8192]{1,0:T(8,128)S(1)} %copy-done.1, f32[4,8,8192]{2,1,0:T(8,128)} %get-tuple-element.29, s32[4,16]{1,0:T(4,128)S(1)} %broadcast_add_fusion, ...), kind=kOutput, calls=%fused_computation.15 | convolution fusion | flops 50988016 | bytes 2884032 | tf_op jit(solution)/shard_map/dot_general | solution.py:557
  124.1 0.4 fusion.8
  124.5 0.7 concatenate.3
  125.2 0.2 add_convert_fusion
  125.4 0.6 constant_dynamic-slice_fusion.grad_ref
  126.1 20.1 %shard_map.164 = (f32[4,8,8,256]{3,2,1,0:T(8,128)}, bf16[16,2048]{1,0:T(8,128)(2,1)}, bf16[16,2048]{1,0:T(8,128)(2,1)}, bf16[16,2048]{1,0:T(8,128)(2,1)}) custom-call(f32[4,8,8,256]{3,2,1,0:T(8,128)} %bitcast.67, bf16[16,2048]{1,0:T(8,128)(2,1)} %bitcast.74, bf16[16,2048]{1,0:T(8,128)(2,1)} %bitcast.72, bf16[16,2048]{1,0:T(8,128)(2,1)} %bitcast.76, ...), custom_call_target="tpu_custom_call" | custom-call | tf_op jit(solution)/shard_map/pallas_call | solution.py:491
  146.2 1.6 %slice.12 = f32[3,4,8,256]{3,0,2,1:T(4,128)} slice(f32[8,4,8,256]{3,0,2,1:T(8,128)} %bitcast.79), slice={[0:3], [0:4], [0:8], [0:256]} | slice | bytes 196608 | tf_op jit(solution)/shard_map/slice | solution.py:508
  147.8 0.7 dynamic-slice_bitcast_fusion
  148.5 0.1 eq.72
  148.6 2.0 %fusion.2 = bf16[1,4,8192]{2,1,0:T(4,128)(2,1)} fusion(bf16[4,8,8192]{2,1,0:T(8,128)(2,1)} %get-tuple-element.27, f32[16,8192]{1,0:T(8,128)S(1)} %convert_element_type.51, s32[]{:T(128)S(6)} %select_n.19, s32[32,16]{1,0:T(8,128)S(1)} %broadcast_bitcast_fusion, pred[32,16]{1,0:T(32,128)(4,1)S(1)} %get-tuple-element.40, s32[32]{0:T(128)S(1)} %eq.72), kind=kOutput, calls=%fused_computation.4 | convolution fusion | flops 2162944 | bytes 724608 | tf_op jit(solution)/shard_map/dot_general | solution.py:518
  150.6 1.5 copy.50
  152.1 1.5 copy.51
  153.5 1.5 copy.52
  (15 shorter events, 0.1 us)
Async XLA Ops:
  0.6 5.3 %copy-start = (f32[3,8192]{1,0:T(4,128)S(1)}, f32[3,8192]{1,0:T(4,128)}, u32[]{:S(2)}) copy-start(f32[3,8192]{1,0:T(4,128)} %param.16) | copy-start | bytes 294916
  40.5 81.6 %copy-start.4 = (f32[16,128]{1,0:T(8,128)S(1)}, f32[16,128]{1,0:T(8,128)}, u32[]{:S(2)}) copy-start(f32[16,128]{1,0:T(8,128)} %get-tuple-element.28) | copy-start | bytes 24580
  40.5 81.7 %copy-start.1 = (f32[16,8192]{1,0:T(8,128)S(1)}, f32[16,8192]{1,0:T(8,128)}, u32[]{:S(2)}) copy-start(f32[16,8192]{1,0:T(8,128)} %fusion.22.gain_ref) | copy-start | bytes 1572868
  40.5 81.7 %copy-start.2 = (bf16[16,8192]{1,0:T(8,128)(2,1)S(1)}, bf16[16,8192]{1,0:T(8,128)(2,1)}, u32[]{:S(2)}) copy-start(bf16[16,8192]{1,0:T(8,128)(2,1)} %get-tuple-element.22) | copy-start | bytes 786436
  40.5 83.6 %copy-start.5 = (s32[1,16]{1,0:T(1,128)S(1)}, s32[1,16]{1,0:T(1,128)}, u32[]{:S(2)}) copy-start(s32[1,16]{1,0:T(1,128)} %param.14) | copy-start | bytes 196
  40.5 84.7 %copy-start.3 = (bf16[1,16,8192]{2,1,0:T(8,128)(2,1)S(1)}, bf16[1,16,8192]{2,1,0:T(8,128)(2,1)}, u32[]{:S(2)}) copy-start(bf16[1,16,8192]{2,1,0:T(8,128)(2,1)} %param.19) | copy-start | bytes 786436
